TPU v7x, 32 devices: a whole 2x2x4 slice. The times are simulated.
32 devices in a mesh: enc: 4 (over z), ctx: 8 (over y, x, core).
Axes of the slice: x: 2, y: 2, z: 4, core: 2. Of those that a mesh axis runs over, the one named last changes fastest.
Arguments:
- patches: bfloat16 [3072, 1280], P('enc'), may hold values from -17 to 17
- patch_image: int32 [3072], P('enc'), may hold values from 63 to 767, as said below
- vit_gain: float32 [1280], replicated, may hold values from 0.1 to 1.9
- vit_qkv: bfloat16 [1280, 16, 240], P(None, 'ctx')
- vit_proj: bfloat16 [1280, 1280], P('ctx'), may hold values from -0.15625 to 0.15625
- merge_gain: float32 [1280], replicated, may hold values from 0.1 to 1.9
- merge_up: bfloat16 [5120, 5120], P(None, 'ctx'), may hold values from -0.078125 to 0.078125
- merge_down: bfloat16 [5120, 8192], P('ctx', 'enc'), may hold values from -0.078125 to 0.078125
- text_embed: bfloat16 [3072, 8192], P('ctx', 'enc'), may hold values from -17 to 17
- placeholder_unit: int32 [3072], replicated, may hold values from -1 to 767, as said below
- doc_id: int32 [3072], replicated, may hold values from 0 to 15, never falling along the last dimension, each value on 1 to 1920 neighbouring positions
- dec_gain: float32 [8192], replicated, may hold values from 0.1 to 1.9
- dec_wq: bfloat16 [8192, 2048], P(None, 'enc')
- dec_wk: bfloat16 [8192, 512], P(None, 'enc')
- dec_wv: bfloat16 [8192, 512], P(None, 'enc'), may hold values from -0.0625 to 0.0625
Outputs:
- attended: bfloat16 [3072, 2048], P('ctx', 'enc')
Inputs may be any that keep to these rules, and one draw needn't show every extreme that they name: `patch_image`: the patches of an image are consecutive, start at a multiple of 4, number a multiple of 4 and at most 256, and lie within one aligned block of 768 patches; image numbers never fall and differ between images; in every such block some image has exactly 256 patches. `placeholder_unit`: -1 marks a text position. Every unit appears exactly once; the units of one image fill consecutive placeholders in their order; the placeholders of an aligned block of 384 positions are consecutive and number at most 192, and some block holds exactly 192. `doc_id`: document numbers never fall; a document has at most 1920 positions, and some document exactly 1920.
All inputs are finite; a program needn't handle non-finite values.
Results may differ from a plain program's by a relative error of at most 0.0085.
Values may be sent and summed in bfloat16 or wider, within the bound.
No kernel may reach another device: no remote copies, remote signals or barrier semaphores. Data moves between devices by JAX's collectives and lax.ppermute only.
A program may use at most 128 MiB of HBM per device.

v0:
```python
import math
import jax
import jax.numpy as jnp
from jax import lax
from jax.sharding import PartitionSpec as P

HD = 128
QPK = 4
EPSILON = 1e-06
NEGATIVE = -1e30


def layer_norm(values, scaling):
    widened = values.astype(jnp.float32)
    center = widened - jnp.mean(widened, axis=1, keepdims=True)
    spread = jnp.mean(center * center, axis=1, keepdims=True)
    return (center * lax.rsqrt(spread + EPSILON) * scaling).astype(jnp.bfloat16)


def image_attention(queries, keys_in, values_in, image_ids):
    head_count, row_count, head_width = queries.shape
    block_rows = math.gcd(row_count, 512)
    scaling = head_width ** (-0.5)

    def image_one_block(offset):
        query_block = lax.dynamic_slice_in_dim(queries, offset, block_rows, 1)
        block_ids = lax.dynamic_slice_in_dim(image_ids, offset, block_rows, 0)
        allowed = block_ids[:, None] == image_ids[None, :]
        scores = (
            jnp.einsum("hqd,hkd->hqk", query_block, keys_in, preferred_element_type=jnp.float32)
            * scaling
        )
        scores = jnp.where(allowed[None], scores, NEGATIVE)
        highest = jnp.max(scores, axis=2, keepdims=True)
        weights = jnp.exp(scores - highest)
        totals = jnp.sum(weights, axis=2, keepdims=True)
        mixture = jnp.einsum(
            "hqk,hkd->hqd",
            weights.astype(jnp.bfloat16),
            values_in,
            preferred_element_type=jnp.float32,
        )
        return (mixture / totals).astype(jnp.bfloat16)

    offsets = jnp.arange(row_count // block_rows, dtype=jnp.int32) * block_rows
    blocks = lax.map(image_one_block, offsets)
    return blocks.transpose(1, 0, 2, 3).reshape(head_count, row_count, head_width)


def body(
    patches,
    patch_image,
    vit_gain,
    vit_qkv,
    vit_proj,
    merge_gain,
    merge_up,
    merge_down,
    text_embed,
    placeholder_unit,
    doc_id,
    dec_gain,
    dec_wq,
    dec_wk,
    dec_wv,
):
    ctx_index = lax.axis_index("ctx")
    group_rows = patches.shape[0]
    head_count = vit_qkv.shape[1]
    head_width = vit_qkv.shape[2] // 3
    normed_patches = layer_norm(patches, vit_gain)
    packed = jnp.dot(
        normed_patches,
        vit_qkv.reshape(vit_qkv.shape[0], head_count * 3 * head_width),
        preferred_element_type=jnp.float32,
    )
    packed = (
        packed.astype(jnp.bfloat16)
        .reshape(group_rows, head_count, 3, head_width)
        .transpose(2, 1, 0, 3)
    )
    attended_patches = image_attention(packed[0], packed[1], packed[2], patch_image)
    flat_heads = attended_patches.transpose(1, 0, 2).reshape(group_rows, head_count * head_width)
    head_terms = jnp.dot(flat_heads, vit_proj, preferred_element_type=jnp.float32)
    summed = lax.psum(head_terms, "ctx")
    vit_out = (patches.astype(jnp.float32) + summed).astype(jnp.bfloat16)
    merge_input = layer_norm(lax.optimization_barrier(vit_out), merge_gain)
    unit_inputs = merge_input.reshape(group_rows // 4, 4 * merge_input.shape[1])
    hidden = jax.nn.gelu(
        jnp.dot(unit_inputs, merge_up, preferred_element_type=jnp.float32), approximate=False
    ).astype(jnp.bfloat16)
    all_hidden = lax.all_gather(hidden, "enc", axis=0, tiled=True)
    unit_total = all_hidden.shape[0]
    tok_rows = text_embed.shape[0]
    local_units = lax.dynamic_slice_in_dim(placeholder_unit, ctx_index * tok_rows, tok_rows, 0)
    present = local_units >= 0
    own_vision = lax.psum_scatter(
        jnp.dot(all_hidden, merge_down, preferred_element_type=jnp.float32),
        "ctx",
        scatter_dimension=0,
        tiled=True,
    ).astype(jnp.bfloat16)
    vision_all = lax.all_gather(own_vision, "ctx", axis=0, tiled=True)
    vision_local = jnp.take(vision_all, jnp.clip(local_units, 0, unit_total - 1), axis=0)
    sequence = jnp.where(present[:, None], vision_local, text_embed)
    full_rows = lax.all_gather(sequence, "enc", axis=1, tiled=True)
    widened = full_rows.astype(jnp.float32)
    row_scale = lax.rsqrt(jnp.mean(widened * widened, axis=1, keepdims=True) + EPSILON)
    normed = (widened * row_scale * dec_gain).astype(jnp.bfloat16)
    queries_flat = jnp.dot(normed, dec_wq, preferred_element_type=jnp.float32).astype(jnp.bfloat16)
    keys_local = jnp.dot(normed, dec_wk, preferred_element_type=jnp.float32).astype(jnp.bfloat16)
    values_local = jnp.dot(normed, dec_wv, preferred_element_type=jnp.float32).astype(jnp.bfloat16)
    kv_local = dec_wk.shape[1] // HD
    queries = queries_flat.reshape(tok_rows, kv_local, QPK, HD).transpose(1, 2, 0, 3)
    query_first = ctx_index * tok_rows
    query_pos = query_first + jnp.arange(tok_rows, dtype=jnp.int32)
    query_docs = lax.dynamic_slice_in_dim(doc_id, query_first, tok_rows, 0)
    scaling = HD ** (-0.5)
    start_state = (
        jnp.full((kv_local, QPK, tok_rows), NEGATIVE, jnp.float32),
        jnp.zeros((kv_local, QPK, tok_rows), jnp.float32),
        jnp.zeros((kv_local, QPK, tok_rows, HD), jnp.float32),
    )
    offset = jnp.int32(0)
    key_part = lax.all_gather(keys_local, "ctx", axis=0, tiled=True)
    value_part = lax.all_gather(values_local, "ctx", axis=0, tiled=True)
    key_count = key_part.shape[0]
    sub_rows = math.gcd(key_count, 512)
    last_doc = lax.dynamic_slice_in_dim(doc_id, offset + key_count - 1, 1, 0)[0]
    visible = (offset <= query_first + tok_rows - 1) & (last_doc >= query_docs[0])

    def update(current):

        def update_one_block(turn_index, inner_state):
            highest, totals, mixture = inner_state
            begin_row = turn_index * sub_rows
            keys_block = lax.dynamic_slice_in_dim(key_part, begin_row, sub_rows, 0).reshape(
                sub_rows, kv_local, HD
            )
            values_block = lax.dynamic_slice_in_dim(value_part, begin_row, sub_rows, 0).reshape(
                sub_rows, kv_local, HD
            )
            key_pos = begin_row + jnp.arange(sub_rows, dtype=jnp.int32)
            key_docs = lax.dynamic_slice_in_dim(doc_id, begin_row, sub_rows, 0)
            allowed = (key_pos[None, :] <= query_pos[:, None]) & (
                key_docs[None, :] == query_docs[:, None]
            )
            scores = (
                jnp.einsum(
                    "gjtd,sgd->gjts", queries, keys_block, preferred_element_type=jnp.float32
                )
                * scaling
            )
            new_peak = jnp.maximum(highest, jnp.max(jnp.where(allowed, scores, NEGATIVE), axis=3))
            factor = jnp.exp(highest - new_peak)
            weights = jnp.where(allowed, jnp.exp(scores - new_peak[..., None]), 0.0)
            totals = totals * factor + jnp.sum(weights, axis=3)
            mixture = mixture * factor[..., None] + jnp.einsum(
                "gjts,sgd->gjtd",
                weights.astype(jnp.bfloat16),
                values_block,
                preferred_element_type=jnp.float32,
            )
            return (new_peak, totals, mixture)

        return lax.fori_loop(0, key_count // sub_rows, update_one_block, current)

    def unchanged(current):
        return current

    finished = lax.cond(visible, update, unchanged, start_state)
    outputs = (finished[2] / finished[1][..., None]).astype(jnp.bfloat16)
    return outputs.transpose(2, 0, 1, 3).reshape(tok_rows, kv_local * QPK * HD)


def solution(mesh):
    placed = (
        P("enc", None),
        P("enc"),
        P(),
        P(None, "ctx", None),
        P("ctx", None),
        P(),
        P(None, "ctx"),
        P("ctx", "enc"),
        P("ctx", "enc"),
        P(),
        P(),
        P(),
        P(None, "enc"),
        P(None, "enc"),
        P(None, "enc"),
    )
    return jax.shard_map(
        body, mesh=mesh, in_specs=placed, out_specs=P("ctx", "enc"), check_vma=False
    )
```

profile of v0, /device:TPU:0, one launch (start us, length us, event | category | flops | bytes accessed | tf_op | source)
XLA Modules:
  0.0 467.7 jit_solution(1278942646428029388)
XLA Ops:
  6.6 2.0 convert_reduce_fusion
  11.7 14.6 %while.28 = (s32[]{:T(128)}, bf16[3,2,256,80]{2,3,1,0:T(8,128)(2,1)}, s32[3]{0:T(128)S(1)}, s32[768]{0:T(1024)S(1)}, bf16[2,768,80]{1,2,0:T(8,128)(2,1)S(1)}, /*...) while((s32[]{:T(128)}, ...), condition=%wide.region_5.6_spmd, body=%wide.region_2.5_spmd.sunk | while | flops 128859136 | bytes 6767287 | solution.py:46
  27.2 2.6 fusion.74
  29.9 80.8 %all-reduce.2.cloned.1.call-done = f32[768,1280]{1,0:T(8,128)} async-done(((f32[768,1280]{1,0:T(8,128)}), f32[768,1280]{1,0:T(8,128)}) %all-reduce.2.cloned.1.call-update) | async-done | bytes 3932176 | tf_op jit(solution)/shard_map/psum | solution.py:85
  110.6 3.1 fusion.50
  114.8 2.0 fusion.49
  116.8 4.1 reshape.149
  120.8 6.1 %fusion.61 = bf16[192,640]{1,0:T(8,128)(2,1)S(1)} fusion(bf16[192,5120]{1,0:T(8,128)(2,1)} %reshape.149, bf16[5120,640]{1,0:T(8,128)(2,1)} %param.27), kind=kOutput, calls=%fused_computation.81 | convolution fusion | flops 1266278400 | bytes 8765440 | tf_op jit(solution)/shard_map/dot_general | solution.py:90
  127.0 21.8 %all_gather.15 = bf16[768,640]{1,0:T(8,128)(2,1)S(1)} all-gather(bf16[192,640]{1,0:T(8,128)(2,1)S(1)} %fusion.61), channel_id=1, replica_groups=mesh['enc'=4,'ctx'=8] {'enc'}, dimensions={0}, use_global_device_ids=true | all-gather | bytes 1228800 | tf_op jit(solution)/shard_map/all_gather | solution.py:92
  148.8 4.5 fusion.75
  153.3 60.7 %reduce-scatter.2.cloned.1.call-done = f32[96,2048]{1,0:T(8,128)} async-done(((f32[768,2048]{1,0:T(8,128)}), f32[96,2048]{1,0:T(8,128)}) %reduce-scatter.2.cloned.1.call-update) | async-done | bytes 786448 | tf_op jit(solution)/shard_map/reduce_scatter | solution.py:97
  214.0 1.9 convert_element_type.68
  217.0 31.3 %all-gather.3.cloned.1.call-done = bf16[768,2048]{1,0:T(8,128)(2,1)} async-done(((bf16[96,2048]{1,0:T(8,128)(2,1)}), bf16[768,2048]{1,0:T(8,128)(2,1)}) %all-gather.3.cloned.1.call-update) | async-done | bytes 3145744 | tf_op jit(solution)/shard_map/all_gather | solution.py:103
  248.3 6.7 %gather_fusion = bf16[384,2048]{1,0:T(8,128)(2,1)S(1)} fusion(bf16[768,2048]{1,0:T(8,128)(2,1)} %all-gather.3.cloned.1.call-done, s32[1024]{0:T(1024)S(1)} %pad_clamp_fusion), kind=kCustom, calls=%fused_computation | custom fusion | bytes 3147264 | tf_op jit(solution)/shard_map/jit(_take)/gather | solution.py:104
  260.3 111.6 %all-gather.5.cloned.1.call-done = bf16[384,8192]{1,0:T(8,128)(2,1)} async-done(((bf16[384,2048]{1,0:T(8,128)(2,1)}), bf16[384,8192]{1,0:T(8,128)(2,1)}) %all-gather.5.cloned.1.call-update) | async-done | bytes 6291472 | tf_op jit(solution)/shard_map/all_gather | solution.py:106
  371.9 4.3 fusion.37
  376.5 3.7 convolution_convert_fusion.1
  380.2 11.4 %all_gather.19 = bf16[3072,128]{1,0:T(8,128)(2,1)} all-gather(bf16[384,128]{1,0:T(8,128)(2,1)S(1)} %convolution_convert_fusion.1), channel_id=1, replica_groups=mesh['enc'=4,'ctx'=8] {'ctx'}, dimensions={0}, use_global_device_ids=true | all-gather | bytes 884736 | tf_op jit(solution)/shard_map/all_gather | solution.py:126
  391.6 3.4 convolution_convert_fusion
  396.0 4.6 convolution_convert_fusion.2
  400.6 11.5 %all_gather.18 = bf16[3072,128]{1,0:T(8,128)(2,1)} all-gather(bf16[384,128]{1,0:T(8,128)(2,1)S(1)} %convolution_convert_fusion.2), channel_id=1, replica_groups=mesh['enc'=4,'ctx'=8] {'ctx'}, dimensions={0}, use_global_device_ids=true | all-gather | bytes 884736 | tf_op jit(solution)/shard_map/all_gather | solution.py:125
  412.2 46.3 %conditional.1 = (f32[1,4,384]{2,1,0:T(4,128)}, f32[1,4,384,128]{3,2,1,0:T(8,128)}) conditional(s32[]{:T(128)} %convert_element_type.60, () %tuple.31, (s32[]{:T(128)}, s32[384]{0:T(512)S(1)}, s32[3072]{0:T(1024)}, s32[384]{0:T(512)S(1)}, bf16[3072,128]{1,0:T(8,128)(2,1)}, /*index=5*/bf16[1,4,384,128]{3,2,1,0:T(8,128)(2,1)}, ...), branch_computations={%region_11.12_spmd, %region_12.17_spmd} | conditional | flops 412493696 | bytes 12566875 | solution.py:171
  412.2 46.3 %while.27 = (s32[]{:T(128)}, f32[1,4,384]{2,1,0:T(4,128)S(1)}, f32[1,4,384]{2,1,0:T(4,128)}, f32[1,4,384,128]{3,2,1,0:T(8,128)}, s32[384]{0:T(512)S(1)}, /*index...) while((s32[]{:T(128)}, f32[1,4,384]{2,1,0:T(4,128)S(1)}, ...), condition=%wide.region_16.16_spmd.clone, body=%wide.region_13.15_spmd.clone.sunk | while | flops 412493312 | bytes 12563663 | solution.py:166
  413.2 1.7 fusion.108
  414.9 2.8 fusion.111
  420.1 1.7 fusion.108
  421.8 3.1 fusion.111
  429.7 3.1 fusion.111
  435.8 1.7 fusion.108
  437.6 3.1 fusion.111
  445.5 3.1 fusion.111
  453.4 3.1 fusion.111
  (136 shorter events, 46.1 us)
Async XLA Ops:
  6.5 142.2 %copy-start = (bf16[640,2048]{1,0:T(8,128)(2,1)S(1)}, bf16[640,2048]{1,0:T(8,128)(2,1)}, u32[]{:S(2)}) copy-start(bf16[640,2048]{1,0:T(8,128)(2,1)} %param.28) | copy-start | bytes 7864324
  6.5 3.0 copy-start.12
  6.5 104.1 %all-reduce.2.cloned.1.call-start = ((), (), s32[]{:S(2)}) async-start(), calls=%async_computation.1 | async-start | bytes 7864320 | tf_op jit(solution)/shard_map/psum | solution.py:85
  6.5 2.3 copy-start.2
  6.6 3.0 copy-start.10
  9.5 2.1 copy-start.7
  11.7 15.5 %copy-start.5 = (bf16[160,1280]{1,0:T(8,128)(2,1)S(1)}, bf16[160,1280]{1,0:T(8,128)(2,1)}, u32[]{:S(2)}) copy-start(bf16[160,1280]{1,0:T(8,128)(2,1)} %param.25) | copy-start | bytes 1228804
  13.9 1.4 copy-start.6
  18.8 1.4 copy-start.6
  23.6 1.4 copy-start.6
  29.8 184.1 %reduce-scatter.2.cloned.1.call-start = ((), (), s32[]{:S(2)}) async-start(), calls=%async_computation.2 | async-start | bytes 7077888 | tf_op jit(solution)/shard_map/reduce_scatter | solution.py:97
  113.8 1.0 copy-start.8
  153.2 95.0 %all-gather.3.cloned.1.call-start = ((), (), s32[]{:S(2)}) async-start(), calls=%async_computation.3 | async-start | bytes 3538944 | tf_op jit(solution)/shard_map/all_gather | solution.py:103
  215.9 156.0 %all-gather.5.cloned.1.call-start = ((), (), s32[]{:S(2)}) async-start(), calls=%async_computation.4 | async-start | bytes 7864320 | tf_op jit(solution)/shard_map/all_gather | solution.py:106
  217.0 38.0 %copy-start.4 = (bf16[384,2048]{1,0:T(8,128)(2,1)S(1)}, bf16[384,2048]{1,0:T(8,128)(2,1)}, u32[]{:S(2)}) copy-start(bf16[384,2048]{1,0:T(8,128)(2,1)} %param.29) | copy-start | bytes 4718596
  256.4 119.8 %copy-start.11 = (f32[8192]{0:T(1024)S(1)}, f32[8192]{0:T(1024)}, u32[]{:S(2)}) copy-start(f32[8192]{0:T(1024)} %param.32) | copy-start | bytes 98308
  371.9 4.6 copy-start.3
  371.9 19.7 %slice-start = ((s8[8388608]{0:T(1024)(128)(4,1)}), s8[4194304]{0:T(1024)(128)(4,1)S(1)}, s32[]{:S(2)}) async-start(s8[8388608]{0:T(1024)(128)(4,1)} %bitcast.126), calls=%async_computation.5 | async-start | bytes 8388608
  376.5 15.1 %slice-start.1 = ((s8[8388608]{0:T(1024)(128)(4,1)}), s8[4194304]{0:T(1024)(128)(4,1)S(1)}, s32[]{:S(2)}) async-start(s8[8388608]{0:T(1024)(128)(4,1)} %bitcast.126), calls=%async_computation.6 | async-start | bytes 8388608
  391.6 4.4 copy-start.9
  458.5 2.7 copy-start.1
Sparse Core Ops, SparseCore 0:
  30.0 80.6 all-reduce.1
  153.4 60.5 reduce-scatter.1
  216.0 32.1 all-gather.2
  256.6 115.3 all-gather.4
where the time goes:
time: 469 us; the launch traced here: 468 us
  waiting for transfers between devices  284 us (61%)
  matrix products  60.8 us (13%)
  blocking collectives  44.7 us (10%)
  other arithmetic  33.3 us (7%)
  local copies, waits for them, and re-layouts  24.3 us (5%)
  between operations  14.6 us (3%)
  loops' own time  5.3 us (1%)
    all_gather x1, waiting for transfers between devices, body(): full_rows = lax.all_gather(sequence, 'enc', axis=1, tiled=True)  112 us
    psum x1, waiting for transfers between devices, body(): summed = lax.psum(head_terms, 'ctx')  80.8 us
    reduce_scatter x1, waiting for transfers between devices, body(): lax.psum_scatter(jnp.dot(all_hidden, merge_down, preferred_element_type=j...  60.7 us
    all_gather x1, waiting for transfers between devices, body(): vision_all = lax.all_gather(own_vision, 'ctx', axis=0, tiled=True)  31.3 us
    all_gather x1, blocking collectives, body(): all_hidden = lax.all_gather(hidden, 'enc', axis=0, tiled=True)  21.8 us
    dot_general x6, matrix products, update_one_block(): jnp.einsum('gjts,sgd->gjtd', weights.astype(jnp.bfloat16), values_block,...  18.4 us
    all_gather x1, blocking collectives, body(): key_part = lax.all_gather(keys_local, 'ctx', axis=0, tiled=True)  11.5 us
    all_gather x1, blocking collectives, body(): value_part = lax.all_gather(values_local, 'ctx', axis=0, tiled=True)  11.4 us
  transfers between devices with their start and end apart: 4, of which 4 were waited for; matrix products, arithmetic and copies ran while one was open for 1% of the time, Pallas kernels for 0%

commit v1 on v0

--- a/solution.py
+++ b/solution.py
@@ -8,6 +8,15 @@
 QPK = 4
 EPSILON = 1e-06
 NEGATIVE = -1e30
+
+
+def add_in_pairs(value, axis):
+    devices = lax.axis_size(axis)
+    summed, far = (value, 1)
+    while far < devices:
+        summed = summed + lax.ppermute(summed, axis, [(i, i ^ far) for i in range(devices)])
+        far = 2 * far
+    return summed
 
 
 def layer_norm(values, scaling):
@@ -82,7 +91,7 @@
     attended_patches = image_attention(packed[0], packed[1], packed[2], patch_image)
     flat_heads = attended_patches.transpose(1, 0, 2).reshape(group_rows, head_count * head_width)
     head_terms = jnp.dot(flat_heads, vit_proj, preferred_element_type=jnp.float32)
-    summed = lax.psum(head_terms, "ctx")
+    summed = add_in_pairs(head_terms, "ctx")
     vit_out = (patches.astype(jnp.float32) + summed).astype(jnp.bfloat16)
     merge_input = layer_norm(lax.optimization_barrier(vit_out), merge_gain)
     unit_inputs = merge_input.reshape(group_rows // 4, 4 * merge_input.shape[1])

time: 469 us -> 567 us (1.21)
  waiting for transfers between devices: 284 us -> 380 us
    ppermute x0 -> x3, waiting for transfers between devices: none -> 176 us  [add_in_pairs(): lax.ppermute(summed, axis, [(i, i ^ far) for i in range(devices)])]
    psum x1 -> x0, waiting for transfers between devices: 80.8 us -> none  [body(): summed = lax.psum(head_terms, 'ctx')]
  transfers between devices with their start and end apart: 4 -> 6, of which waited for: 4 -> 6; matrix products, arithmetic and copies ran while one was open for 1% -> 1% of each run, Pallas kernels for 0% -> 0%
where the time goes in v1:
time: 567 us; the launch traced here: 566 us
  waiting for transfers between devices  380 us (67%)
  matrix products  59.1 us (10%)
  blocking collectives  45.1 us (8%)
  other arithmetic  31.8 us (6%)
  local copies, waits for them, and re-layouts  24.3 us (4%)
  between operations  14.6 us (3%)
  loops' own time  5.88 us (1%)
    ppermute x3, waiting for transfers between devices, add_in_pairs(): lax.ppermute(summed, axis, [(i, i ^ far) for i in range(devices)])  176 us
    all_gather x1, waiting for transfers between devices, body(): full_rows = lax.all_gather(sequence, 'enc', axis=1, tiled=True)  112 us
    reduce_scatter x1, waiting for transfers between devices, body(): lax.psum_scatter(jnp.dot(all_hidden, merge_down, preferred_element_type=j...  60.4 us
    all_gather x1, waiting for transfers between devices, body(): vision_all = lax.all_gather(own_vision, 'ctx', axis=0, tiled=True)  31.5 us
    all_gather x1, blocking collectives, body(): all_hidden = lax.all_gather(hidden, 'enc', axis=0, tiled=True)  22.2 us
    dot_general x6, matrix products, update_one_block(): jnp.einsum('gjts,sgd->gjtd', weights.astype(jnp.bfloat16), values_block,...  18.5 us
    all_gather x1, blocking collectives, body(): value_part = lax.all_gather(values_local, 'ctx', axis=0, tiled=True)  11.6 us
  transfers between devices with their start and end apart: 6, of which 6 were waited for; matrix products, arithmetic and copies ran while one was open for 1% of the time, Pallas kernels for 0%

profile of v1, /device:TPU:0, one launch (start us, length us, event | category | flops | bytes accessed | tf_op | source)
XLA Modules:
  0.0 566.1 jit_solution(14935729042227969305)
XLA Ops:
  6.6 2.0 convert_reduce_fusion
  11.7 15.2 %while.28 = (s32[]{:T(128)}, bf16[3,2,256,80]{2,3,1,0:T(8,128)(2,1)}, s32[3]{0:T(128)S(1)}, s32[768]{0:T(1024)S(1)}, bf16[2,768,80]{1,2,0:T(8,128)(2,1)S(1)}, /*...) while((s32[]{:T(128)}, ...), condition=%wide.region_5.6_spmd, body=%wide.region_2.5_spmd.sunk | while | flops 128859136 | bytes 6767287 | solution.py:55
  29.1 6.4 %collective-permute-done = f32[768,1280]{1,0:T(8,128)S(1)} collective-permute-done((f32[768,1280]{1,0:T(8,128)S(1)}, f32[768,1280]{1,0:T(8,128)S(1)}, u32[]{:S(2)}, u32[]{:S(2)}) %collective-permute-start) | collective-permute-done | bytes 3932192 | tf_op jit(solution)/shard_map/ppermute | solution.py:17
  36.0 2.9 collective-permute-start.1
  38.9 85.3 %collective-permute-done.1 = f32[768,1280]{1,0:T(8,128)S(1)} collective-permute-done((f32[768,1280]{1,0:T(8,128)S(1)}, f32[768,1280]{1,0:T(8,128)S(1)}, u32[]{:S(2)}, u32[]{:S(2)}) %collective-permute-start.1) | collective-permute-done | bytes 3932192 | tf_op jit(solution)/shard_map/ppermute | solution.py:17
  124.7 1.8 collective-permute-start.2
  126.5 84.6 %collective-permute-done.2 = f32[768,1280]{1,0:T(8,128)S(1)} collective-permute-done((f32[768,1280]{1,0:T(8,128)S(1)}, f32[768,1280]{1,0:T(8,128)S(1)}, u32[]{:S(2)}, u32[]{:S(2)}) %collective-permute-start.2) | collective-permute-done | bytes 3932192 | tf_op jit(solution)/shard_map/ppermute | solution.py:17
  212.9 2.0 fusion.49
  214.9 4.1 reshape.149
  218.9 6.1 %fusion.61 = bf16[192,640]{1,0:T(8,128)(2,1)S(1)} fusion(bf16[192,5120]{1,0:T(8,128)(2,1)} %reshape.149, bf16[5120,640]{1,0:T(8,128)(2,1)} %param.27), kind=kOutput, calls=%fused_computation.81 | convolution fusion | flops 1266278400 | bytes 8765440 | tf_op jit(solution)/shard_map/dot_general | solution.py:99
  225.1 22.2 %all_gather.15 = bf16[768,640]{1,0:T(8,128)(2,1)S(1)} all-gather(bf16[192,640]{1,0:T(8,128)(2,1)S(1)} %fusion.61), channel_id=1, replica_groups=mesh['enc'=4,'ctx'=8] {'enc'}, dimensions={0}, use_global_device_ids=true | all-gather | bytes 1228800 | tf_op jit(solution)/shard_map/all_gather | solution.py:101
  247.3 4.5 fusion.75
  251.9 60.4 %reduce-scatter.2.cloned.1.call-done = f32[96,2048]{1,0:T(8,128)} async-done(((f32[768,2048]{1,0:T(8,128)}), f32[96,2048]{1,0:T(8,128)}) %reduce-scatter.2.cloned.1.call-update) | async-done | bytes 786448 | tf_op jit(solution)/shard_map/reduce_scatter | solution.py:106
  312.3 1.9 convert_element_type.68
  315.1 31.5 %all-gather.3.cloned.1.call-done = bf16[768,2048]{1,0:T(8,128)(2,1)} async-done(((bf16[96,2048]{1,0:T(8,128)(2,1)}), bf16[768,2048]{1,0:T(8,128)(2,1)}) %all-gather.3.cloned.1.call-update) | async-done | bytes 3145744 | tf_op jit(solution)/shard_map/all_gather | solution.py:112
  346.6 6.7 %gather_fusion = bf16[384,2048]{1,0:T(8,128)(2,1)S(1)} fusion(bf16[768,2048]{1,0:T(8,128)(2,1)} %all-gather.3.cloned.1.call-done, s32[1024]{0:T(1024)S(1)} %pad_clamp_fusion), kind=kCustom, calls=%fused_computation | custom fusion | bytes 3147264 | tf_op jit(solution)/shard_map/jit(_take)/gather | solution.py:113
  358.6 111.6 %all-gather.5.cloned.1.call-done = bf16[384,8192]{1,0:T(8,128)(2,1)} async-done(((bf16[384,2048]{1,0:T(8,128)(2,1)}), bf16[384,8192]{1,0:T(8,128)(2,1)}) %all-gather.5.cloned.1.call-update) | async-done | bytes 6291472 | tf_op jit(solution)/shard_map/all_gather | solution.py:115
  470.2 4.3 fusion.37
  474.8 3.7 convolution_convert_fusion.1
  478.5 11.6 %all_gather.19 = bf16[3072,128]{1,0:T(8,128)(2,1)} all-gather(bf16[384,128]{1,0:T(8,128)(2,1)S(1)} %convolution_convert_fusion.1), channel_id=1, replica_groups=mesh['enc'=4,'ctx'=8] {'ctx'}, dimensions={0}, use_global_device_ids=true | all-gather | bytes 884736 | tf_op jit(solution)/shard_map/all_gather | solution.py:135
  490.2 3.5 convolution_convert_fusion
  494.5 4.6 convolution_convert_fusion.2
  499.2 11.3 %all_gather.18 = bf16[3072,128]{1,0:T(8,128)(2,1)} all-gather(bf16[384,128]{1,0:T(8,128)(2,1)S(1)} %convolution_convert_fusion.2), channel_id=1, replica_groups=mesh['enc'=4,'ctx'=8] {'ctx'}, dimensions={0}, use_global_device_ids=true | all-gather | bytes 884736 | tf_op jit(solution)/shard_map/all_gather | solution.py:134
  510.5 46.4 %conditional.1 = (f32[1,4,384]{2,1,0:T(4,128)}, f32[1,4,384,128]{3,2,1,0:T(8,128)}) conditional(s32[]{:T(128)} %convert_element_type.60, () %tuple.31, (s32[]{:T(128)}, s32[384]{0:T(512)S(1)}, s32[3072]{0:T(1024)}, s32[384]{0:T(512)S(1)}, bf16[3072,128]{1,0:T(8,128)(2,1)}, /*index=5*/bf16[1,4,384,128]{3,2,1,0:T(8,128)(2,1)}, ...), branch_computations={%region_10.11_spmd, %region_11.16_spmd} | conditional | flops 412493696 | bytes 12566875 | solution.py:180
  510.5 46.4 %while.27 = (s32[]{:T(128)}, f32[1,4,384]{2,1,0:T(4,128)S(1)}, f32[1,4,384]{2,1,0:T(4,128)}, f32[1,4,384,128]{3,2,1,0:T(8,128)}, s32[384]{0:T(512)S(1)}, /*index...) while((s32[]{:T(128)}, f32[1,4,384]{2,1,0:T(4,128)S(1)}, ...), condition=%wide.region_15.15_spmd.clone, body=%wide.region_12.14_spmd.clone.sunk | while | flops 412493312 | bytes 12563663 | solution.py:175
  513.3 2.8 fusion.111
  520.2 3.1 fusion.111
  528.0 3.1 fusion.111
  535.9 3.1 fusion.111
  542.0 1.7 fusion.108
  543.8 3.1 fusion.111
  551.7 3.1 fusion.111
  (143 shorter events, 52.3 us)
Async XLA Ops:
  6.5 240.8 %copy-start = (bf16[640,2048]{1,0:T(8,128)(2,1)S(1)}, bf16[640,2048]{1,0:T(8,128)(2,1)}, u32[]{:S(2)}) copy-start(bf16[640,2048]{1,0:T(8,128)(2,1)} %param.28) | copy-start | bytes 7864324
  6.5 3.0 copy-start.13
  6.5 305.7 %reduce-scatter.2.cloned.1.call-start = ((), (), s32[]{:S(2)}) async-start(), calls=%async_computation.1 | async-start | bytes 7077888 | tf_op jit(solution)/shard_map/reduce_scatter | solution.py:106
  6.5 2.3 copy-start.2
  6.6 3.0 copy-start.11
  9.5 2.1 copy-start.8
  11.7 16.1 %copy-start.6 = (bf16[160,1280]{1,0:T(8,128)(2,1)S(1)}, bf16[160,1280]{1,0:T(8,128)(2,1)}, u32[]{:S(2)}) copy-start(bf16[160,1280]{1,0:T(8,128)(2,1)} %param.25) | copy-start | bytes 1228804
  14.1 1.4 copy-start.7
  19.2 1.4 copy-start.7
  24.3 1.4 copy-start.7
  28.6 7.0 %collective-permute-start = (f32[768,1280]{1,0:T(8,128)S(1)}, f32[768,1280]{1,0:T(8,128)S(1)}, u32[]{:S(2)}, u32[]{:S(2)}) collective-permute-start(f32[768,1280]{1,0:T(8,128)S(1)} %fusion.74), channel_id=1, source_target_pairs={{0,1},{1,0},{2,3},{3,2},{4,5},{5,4},{6,7},{7,6},{8,9},{9,8},{10,11... | collective-permute-start | bytes 11796488 | tf_op jit(solution)/shard_map/ppermute | solution.py:17
  36.0 175.2 %copy-start.3 = (bf16[768,1280]{1,0:T(8,128)(2,1)S(1)}, bf16[768,1280]{1,0:T(8,128)(2,1)}, u32[]{:S(2)}) copy-start(bf16[768,1280]{1,0:T(8,128)(2,1)} %param.21) | copy-start | bytes 5898244
  36.0 88.2 %collective-permute-start.1 = (f32[768,1280]{1,0:T(8,128)S(1)}, f32[768,1280]{1,0:T(8,128)S(1)}, u32[]{:S(2)}, u32[]{:S(2)}) collective-permute-start(f32[768,1280]{1,0:T(8,128)S(1)} %add.131), channel_id=1, source_target_pairs={{0,2},{1,3},{2,0},{3,1},{4,6},{5,7},{6,4},{7,5},{8,10},{9,11},{10,... | collective-permute-start | bytes 11796488 | tf_op jit(solution)/shard_map/ppermute | solution.py:17
  124.7 86.5 %collective-permute-start.2 = (f32[768,1280]{1,0:T(8,128)S(1)}, f32[768,1280]{1,0:T(8,128)S(1)}, u32[]{:S(2)}, u32[]{:S(2)}) collective-permute-start(f32[768,1280]{1,0:T(8,128)S(1)} %add.132), channel_id=1, source_target_pairs={{0,4},{1,5},{2,6},{3,7},{4,0},{5,1},{6,2},{7,3},{8,12},{9,13},{10,... | collective-permute-start | bytes 11796488 | tf_op jit(solution)/shard_map/ppermute | solution.py:17
  211.9 1.0 copy-start.9
  251.8 94.7 %all-gather.3.cloned.1.call-start = ((), (), s32[]{:S(2)}) async-start(), calls=%async_computation.2 | async-start | bytes 3538944 | tf_op jit(solution)/shard_map/all_gather | solution.py:112
  314.2 156.0 %all-gather.5.cloned.1.call-start = ((), (), s32[]{:S(2)}) async-start(), calls=%async_computation.3 | async-start | bytes 7864320 | tf_op jit(solution)/shard_map/all_gather | solution.py:115
  315.1 38.2 %copy-start.5 = (bf16[384,2048]{1,0:T(8,128)(2,1)S(1)}, bf16[384,2048]{1,0:T(8,128)(2,1)}, u32[]{:S(2)}) copy-start(bf16[384,2048]{1,0:T(8,128)(2,1)} %param.29) | copy-start | bytes 4718596
  354.7 119.8 %copy-start.12 = (f32[8192]{0:T(1024)S(1)}, f32[8192]{0:T(1024)}, u32[]{:S(2)}) copy-start(f32[8192]{0:T(1024)} %param.32) | copy-start | bytes 98308
  470.2 4.6 copy-start.4
  470.2 19.9 %slice-start = ((s8[8388608]{0:T(1024)(128)(4,1)}), s8[4194304]{0:T(1024)(128)(4,1)S(1)}, s32[]{:S(2)}) async-start(s8[8388608]{0:T(1024)(128)(4,1)} %bitcast.126), calls=%async_computation.4 | async-start | bytes 8388608
  474.8 15.3 %slice-start.1 = ((s8[8388608]{0:T(1024)(128)(4,1)}), s8[4194304]{0:T(1024)(128)(4,1)S(1)}, s32[]{:S(2)}) async-start(s8[8388608]{0:T(1024)(128)(4,1)} %bitcast.126), calls=%async_computation.5 | async-start | bytes 8388608
  490.2 4.4 copy-start.10
  556.8 2.7 copy-start.1
Sparse Core Ops, SparseCore 0:
  252.0 60.2 reduce-scatter.1
  314.3 32.1 all-gather.2
  354.9 115.3 all-gather.4
